TPU v7x, 32 devices: a whole 2x2x4 slice. The times are simulated.
32 devices in a mesh: row: 4 (over y, core), col: 8 (over z, x).
Axes of the slice: x: 2, y: 2, z: 4, core: 2. Of those that a mesh axis runs over, the one named last changes fastest.
Arguments:
- matrix: float32 [16384, 16384], P('row', 'col'), as said below
Outputs:
- updated: float32 [16384, 16384], P('row', 'col')
- reflectors: float32 [1, 16384, 256], P(None, ('row', 'col'))
- products: float32 [1, 16384, 256], P(None, ('row', 'col'))
Inputs may be any that keep to these rules, and one draw needn't show every extreme that they name: `matrix`: symmetric.
All inputs are finite; a program needn't handle non-finite values.
Results may differ from a plain program's by a relative error of at most 0.0003.
Values sent between devices are 32-bit elements; how exact they have to be, the bound alone decides.
A program may use at most 192 MiB of HBM per device.

v0:
```python
import jax
import jax.numpy as jnp
from jax import lax
from jax.sharding import PartitionSpec as P

NB = 256


leaf_width = 16


def spread(value, axis, source):
    kept = jnp.where(lax.axis_index(axis) == source, value, 0).astype(value.dtype)
    return lax.psum(kept, axis)


def matmul(left, right):
    return jnp.dot(left, right, precision=lax.Precision.HIGHEST, preferred_element_type=jnp.float32)


def lu_signed(square):
    order_n = square.shape[0]
    width = min(leaf_width, order_n)
    all_ids = jnp.arange(order_n)
    panel_ids = jnp.arange(width)
    work_mat = square
    sign_vec = jnp.zeros((order_n,), jnp.float32)
    for first in range(0, order_n, width):
        panel = work_mat[:, first : first + width]

        def leaf_step(local_idx, state, first=first):
            panel, sign_vec = state
            pivot_idx = first + local_idx
            column = lax.dynamic_slice_in_dim(panel, local_idx, 1, 1)[:, 0]
            raw_pivot = column[pivot_idx]
            sign_now = jnp.where(raw_pivot >= 0, 1.0, -1.0).astype(jnp.float32)
            pivot_val = raw_pivot + sign_now
            lower_col = jnp.where(all_ids > pivot_idx, column / pivot_val, 0.0)
            upper_row = jnp.where(panel_ids > local_idx, panel[pivot_idx, :], 0.0)
            panel = panel - lower_col[:, None] * upper_row[None, :]
            kept = jnp.where(
                all_ids > pivot_idx, lower_col, jnp.where(all_ids == pivot_idx, pivot_val, column)
            )
            panel = lax.dynamic_update_slice_in_dim(panel, kept[:, None], local_idx, 1)
            sign_vec = sign_vec.at[pivot_idx].set(sign_now)
            return (panel, sign_vec)

        panel, sign_vec = lax.fori_loop(0, width, leaf_step, (panel, sign_vec))
        work_mat = work_mat.at[:, first : first + width].set(panel)
        after = first + width
        if after < order_n:
            diag_lower = jnp.tril(panel[first:after], -1) + jnp.eye(width, dtype=jnp.float32)
            upper_right = jax.scipy.linalg.solve_triangular(
                diag_lower, work_mat[first:after, after:], lower=True, unit_diagonal=True
            )
            trailing = work_mat[after:, after:] - matmul(panel[after:], upper_right)
            work_mat = work_mat.at[first:after, after:].set(upper_right)
            work_mat = work_mat.at[after:, after:].set(trailing)
    unit_lower = jnp.tril(work_mat, -1) + jnp.eye(order_n, dtype=jnp.float32)
    return (unit_lower, jnp.triu(work_mat), sign_vec)


def body(matrix):
    row_count, col_count = matrix.shape
    row_index = lax.axis_index("row")
    col_index = lax.axis_index("col")
    col_devices = lax.axis_size("col")
    share_rows = row_count // col_devices
    row_ids = row_index * row_count + jnp.arange(row_count)
    owner_row = col_index * col_count // row_count
    owner_offset = col_index * col_count % row_count
    current = matrix
    row_start = NB
    panel_cols = lax.slice_in_dim(current, 0, NB, axis=1)
    panel_cols = spread(panel_cols, "col", 0)
    panel_cols = jnp.where((row_ids >= row_start)[:, None], panel_cols, 0.0)
    gram_sum = lax.psum(matmul(panel_cols.T, panel_cols), "row")
    chol_low = jnp.linalg.cholesky(gram_sum)
    q_basis = jax.scipy.linalg.solve_triangular(chol_low, panel_cols.T, lower=True).T
    top_block = spread(q_basis[row_start : row_start + NB], "row", 0)
    unit_lower, upper_tri, sign_diag = lu_signed(top_block)
    solved = jax.scipy.linalg.solve_triangular(upper_tri.T, q_basis.T, lower=True).T
    rel_pos = row_ids - row_start
    in_top = (rel_pos >= 0) & (rel_pos < NB)
    lower_rows = jnp.take(unit_lower, jnp.clip(rel_pos, 0, NB - 1), axis=0)
    refl = jnp.where(in_top[:, None], lower_rows, jnp.where((rel_pos < 0)[:, None], 0.0, solved))
    scaled = upper_tri * sign_diag[None, :]
    t_factor = jax.scipy.linalg.solve_triangular(
        unit_lower, scaled.T, lower=True, unit_diagonal=True
    ).T
    own_slice = lax.dynamic_slice_in_dim(refl, owner_offset, col_count, 0)
    refl_cols = spread(own_slice, "row", owner_row)
    x_rows = lax.psum(matmul(current, matmul(refl_cols, t_factor)), "col")
    inner_prod = lax.psum(matmul(refl.T, x_rows), "row")
    correction = matmul(t_factor.T, inner_prod)
    w_rows = x_rows - 0.5 * matmul(refl, correction)
    x_cols = lax.psum(matmul(current.T, matmul(refl, t_factor)), "row")
    w_cols = x_cols - 0.5 * matmul(refl_cols, correction)
    left_pair = jnp.concatenate([refl, w_rows], axis=1)
    right_pair = jnp.concatenate([w_cols, refl_cols], axis=1)
    current = current - matmul(left_pair, right_pair.T)
    all_refl = [lax.dynamic_slice_in_dim(refl, col_index * share_rows, share_rows, 0)]
    all_prod = [lax.dynamic_slice_in_dim(w_rows, col_index * share_rows, share_rows, 0)]
    return (current, jnp.stack(all_refl), jnp.stack(all_prod))


def solution(mesh):
    return jax.shard_map(
        body,
        mesh=mesh,
        in_specs=(P("row", "col"),),
        out_specs=(P("row", "col"), P(None, ("row", "col"), None), P(None, ("row", "col"), None)),
        check_vma=False,
    )
```

profile of v0, /device:TPU:0, one launch (start us, length us, event | category | flops | bytes accessed | tf_op | source)
XLA Modules:
  0.0 1536.8 jit_solution(7830137127578075882)
XLA Ops:
  7.2 4.5 slice_select_fusion
  12.6 158.8 %all-reduce.9.cloned.1.call-done = f32[4096,256]{1,0:T(8,128)} async-done(((f32[4096,256]{1,0:T(8,128)}), f32[4096,256]{1,0:T(8,128)}) %all-reduce.9.cloned.1.call-update) | async-done | bytes 4194320 | tf_op jit(solution)/shard_map/psum | solution.py:14
  171.4 12.2 fusion.89
  184.1 3.9 select_bitcast_fusion
  188.1 27.0 %all-reduce.11.cloned.1.call-done = f32[256,256]{0,1:T(8,128)} async-done(((f32[256,256]{0,1:T(8,128)}), f32[256,256]{0,1:T(8,128)}) %all-reduce.11.cloned.1.call-update) | async-done | bytes 262160 | tf_op jit(solution)/shard_map/psum | solution.py:77
  217.1 11.7 cholesky.50
  228.9 9.8 custom-call.78
  239.2 11.7 cholesky.105
  253.1 4.0 while.404
  257.0 19.8 %custom-call.96 = f32[2,128,128]{1,2,0:T(8,128)S(1)} custom-call(f32[2,128,128]{2,1,0:T(8,128)S(1)} %get-tuple-element.3807), custom_call_target="InvertDiagBlocksLowerTriangular" | custom-call | tf_op jit(solution)/shard_map/jit(_solve_triangular)/triangular_solve | solution.py:79
  276.9 3.7 fusion.92
  280.6 4.8 convolution_subtract_fusion.2
  287.2 3.5 fusion.110
  303.5 22.0 %all-reduce.13.cloned.1.call-done = f32[256,256]{1,0:T(8,128)} async-done(((f32[256,256]{1,0:T(8,128)}), f32[256,256]{1,0:T(8,128)}) %all-reduce.13.cloned.1.call-update) | async-done | bytes 262160 | tf_op jit(solution)/shard_map/psum | solution.py:14
  326.5 37.1 %while.388 = (s32[]{:T(128)}, f32[256,16]{0,1:T(8,128)S(1)}, f32[256]{0:T(256)S(1)}, s32[]{:T(128)}, s32[]{:T(128)}, /*index=5*/s32[]{:T(128)}, s32[]{:T(128)}, f32[]{:T(128)}, f32[]{:T(128)}, f32[]{:T(128)}) while((s32[]{:T(128)}, f32[256,16]{0,1:T(8,128)S(1)}, f32[256]{0:T(256)S(1)}, s32[]{:T(128)}, s32[]{:T(128)}, ...), condition=%wide.region_9.11_spmd.clone.clone, body=%wide.region_8.10_spmd.clone.clone.sunk | while | flops 9771 | bytes 75169 | solution.py:48
  379.3 37.1 %while.389 = (s32[]{:T(128)}, f32[256,16]{0,1:T(8,128)S(1)}, f32[256]{0:T(256)S(1)}, s32[]{:T(128)}, s32[]{:T(128)}, /*index=5*/s32[]{:T(128)}, s32[]{:T(128)}, ...) while((s32[]{:T(128)}, f32[256,16]{0,1:T(8,128)S(1)}, ...), condition=%wide.region_13.15_spmd.clone.clone, body=%wide.region_12.14_spmd.clone.clone.sunk | while | flops 9775 | bytes 74215 | solution.py:48
  429.4 37.1 %while.390 = (s32[]{:T(128)}, f32[256,16]{0,1:T(8,128)S(1)}, f32[256]{0:T(256)S(1)}, s32[]{:T(128)}, s32[]{:T(128)}, /*index=5*/s32[]{:T(128)}, s32[]{:T(128)}, ...) while((s32[]{:T(128)}, f32[256,16]{0,1:T(8,128)S(1)}, ...), condition=%wide.region_16.18_spmd.clone.clone, body=%wide.region_15.17_spmd.clone.clone.sunk | while | flops 9775 | bytes 74215 | solution.py:48
  479.4 37.1 %while.391 = (s32[]{:T(128)}, f32[256,16]{0,1:T(8,128)S(1)}, f32[256]{0:T(256)S(1)}, s32[]{:T(128)}, s32[]{:T(128)}, /*index=5*/s32[]{:T(128)}, s32[]{:T(128)}, ...) while((s32[]{:T(128)}, f32[256,16]{0,1:T(8,128)S(1)}, ...), condition=%wide.region_19.21_spmd.clone.clone, body=%wide.region_18.20_spmd.clone.clone.sunk | while | flops 9775 | bytes 74215 | solution.py:48
  529.3 37.1 %while.392 = (s32[]{:T(128)}, f32[256,16]{0,1:T(8,128)S(1)}, f32[256]{0:T(256)S(1)}, s32[]{:T(128)}, s32[]{:T(128)}, /*index=5*/s32[]{:T(128)}, s32[]{:T(128)}, ...) while((s32[]{:T(128)}, f32[256,16]{0,1:T(8,128)S(1)}, ...), condition=%wide.region_22.24_spmd.clone.clone, body=%wide.region_21.23_spmd.clone.clone.sunk | while | flops 9775 | bytes 74215 | solution.py:48
  579.1 37.1 %while.393 = (s32[]{:T(128)}, f32[256,16]{0,1:T(8,128)S(1)}, f32[256]{0:T(256)S(1)}, s32[]{:T(128)}, s32[]{:T(128)}, /*index=5*/s32[]{:T(128)}, s32[]{:T(128)}, ...) while((s32[]{:T(128)}, f32[256,16]{0,1:T(8,128)S(1)}, ...), condition=%wide.region_25.27_spmd.clone.clone, body=%wide.region_24.26_spmd.clone.clone.sunk | while | flops 9775 | bytes 74215 | solution.py:48
  628.9 37.1 %while.394 = (s32[]{:T(128)}, f32[256,16]{0,1:T(8,128)S(1)}, f32[256]{0:T(256)S(1)}, s32[]{:T(128)}, s32[]{:T(128)}, /*index=5*/s32[]{:T(128)}, s32[]{:T(128)}, ...) while((s32[]{:T(128)}, f32[256,16]{0,1:T(8,128)S(1)}, ...), condition=%wide.region_28.30_spmd.clone.clone, body=%wide.region_27.29_spmd.clone.clone.sunk | while | flops 9775 | bytes 74215 | solution.py:48
  679.1 37.1 %while.395 = (s32[]{:T(128)}, f32[256,16]{0,1:T(8,128)S(1)}, f32[256]{0:T(256)S(1)}, s32[]{:T(128)}, s32[]{:T(128)}, /*index=5*/s32[]{:T(128)}, s32[]{:T(128)}, ...) while((s32[]{:T(128)}, f32[256,16]{0,1:T(8,128)S(1)}, ...), condition=%wide.region_31.33_spmd.clone.clone, body=%wide.region_30.32_spmd.clone.clone.sunk | while | flops 9775 | bytes 74215 | solution.py:48
  724.2 37.1 %while.396 = (s32[]{:T(128)}, f32[256,16]{0,1:T(8,128)S(1)}, f32[256]{0:T(256)S(1)}, s32[]{:T(128)}, s32[]{:T(128)}, /*index=5*/s32[]{:T(128)}, s32[]{:T(128)}, ...) while((s32[]{:T(128)}, f32[256,16]{0,1:T(8,128)S(1)}, ...), condition=%wide.region_34.36_spmd.clone.clone, body=%wide.region_33.35_spmd.clone.clone.sunk | while | flops 9775 | bytes 74215 | solution.py:48
  766.9 37.1 %while.397 = (s32[]{:T(128)}, f32[256,16]{0,1:T(8,128)S(1)}, f32[256]{0:T(256)S(1)}, s32[]{:T(128)}, s32[]{:T(128)}, /*index=5*/s32[]{:T(128)}, s32[]{:T(128)}, ...) while((s32[]{:T(128)}, f32[256,16]{0,1:T(8,128)S(1)}, ...), condition=%wide.region_37.39_spmd.clone.clone, body=%wide.region_36.38_spmd.clone.clone.sunk | while | flops 9775 | bytes 74215 | solution.py:48
  809.7 37.1 %while.398 = (s32[]{:T(128)}, f32[256,16]{0,1:T(8,128)S(1)}, f32[256]{0:T(256)S(1)}, s32[]{:T(128)}, s32[]{:T(128)}, /*index=5*/s32[]{:T(128)}, s32[]{:T(128)}, ...) while((s32[]{:T(128)}, f32[256,16]{0,1:T(8,128)S(1)}, ...), condition=%wide.region_40.42_spmd.clone.clone, body=%wide.region_39.41_spmd.clone.clone.sunk | while | flops 9775 | bytes 74215 | solution.py:48
  852.5 37.1 %while.399 = (s32[]{:T(128)}, f32[256,16]{0,1:T(8,128)S(1)}, f32[256]{0:T(256)S(1)}, s32[]{:T(128)}, s32[]{:T(128)}, /*index=5*/s32[]{:T(128)}, s32[]{:T(128)}, ...) while((s32[]{:T(128)}, f32[256,16]{0,1:T(8,128)S(1)}, ...), condition=%wide.region_43.45_spmd.clone.clone, body=%wide.region_42.44_spmd.clone.clone.sunk | while | flops 9775 | bytes 74215 | solution.py:48
  895.1 37.1 %while.400 = (s32[]{:T(128)}, f32[256,16]{0,1:T(8,128)S(1)}, f32[256]{0:T(256)S(1)}, s32[]{:T(128)}, s32[]{:T(128)}, /*index=5*/s32[]{:T(128)}, s32[]{:T(128)}, ...) while((s32[]{:T(128)}, f32[256,16]{0,1:T(8,128)S(1)}, ...), condition=%wide.region_46.48_spmd.clone.clone, body=%wide.region_45.47_spmd.clone.clone.sunk | while | flops 9775 | bytes 74215 | solution.py:48
  937.8 37.1 %while.401 = (s32[]{:T(128)}, f32[256,16]{0,1:T(8,128)S(1)}, f32[256]{0:T(256)S(1)}, s32[]{:T(128)}, s32[]{:T(128)}, /*index=5*/s32[]{:T(128)}, s32[]{:T(128)}, ...) while((s32[]{:T(128)}, f32[256,16]{0,1:T(8,128)S(1)}, ...), condition=%wide.region_49.51_spmd.clone.clone, body=%wide.region_48.50_spmd.clone.clone.sunk | while | flops 9775 | bytes 74215 | solution.py:48
  980.3 37.1 %while.402 = (s32[]{:T(128)}, f32[256,16]{0,1:T(8,128)S(1)}, f32[256]{0:T(256)S(1)}, s32[]{:T(128)}, s32[]{:T(128)}, /*index=5*/s32[]{:T(128)}, s32[]{:T(128)}, ...) while((s32[]{:T(128)}, f32[256,16]{0,1:T(8,128)S(1)}, ...), condition=%wide.region_52.54_spmd.clone.clone, body=%wide.region_51.53_spmd.clone.clone.sunk | while | flops 9775 | bytes 74215 | solution.py:48
  1022.7 37.1 %while.403 = (s32[]{:T(128)}, f32[256,16]{0,1:T(8,128)S(1)}, f32[256]{0:T(256)S(1)}, s32[]{:T(128)}, s32[]{:T(128)}, /*index=5*/s32[]{:T(128)}, s32[]{:T(128)}, ...) while((s32[]{:T(128)}, f32[256,16]{0,1:T(8,128)S(1)}, ...), condition=%wide.region_54.56_spmd.clone.clone, body=%wide.region_53.55_spmd.clone.clone.sunk | while | flops 9775 | bytes 74215 | solution.py:48
  1061.0 16.1 %gather_fusion = f32[4096,256]{1,0:T(8,128)} fusion(f32[256,256]{1,0:T(8,128)S(1)} %get-tuple-element.4059, s32[4096]{0:T(1024)S(1)} %broadcast_clamp_fusion), kind=kCustom, calls=%fused_computation | custom fusion | bytes 8404992 | tf_op jit(solution)/shard_map/jit(_take)/gather | solution.py:85
  1077.2 5.6 copy.109
  1082.8 4.2 while.405
  1087.0 19.9 %custom-call.97 = f32[2,128,128]{1,2,0:T(8,128)S(1)} custom-call(f32[2,128,128]{2,1,0:T(8,128)S(1)} %get-tuple-element.3808), custom_call_target="InvertDiagBlocksLowerTriangular" | custom-call | tf_op jit(solution)/shard_map/jit(_solve_triangular)/triangular_solve | solution.py:82
  1108.9 3.6 convolution_subtract_fusion.1
  1119.0 4.3 while.387
  1123.3 19.7 %custom-call.94 = f32[2,128,128]{1,2,0:T(8,128)S(1)} custom-call(f32[2,128,128]{2,1,0:T(8,128)S(1)} %get-tuple-element.3432), custom_call_target="InvertDiagBlocksLowerTriangular" | custom-call | tf_op jit(solution)/shard_map/jit(_solve_triangular)/triangular_solve | solution.py:88
  1144.0 26.6 %all-reduce.15.cloned.1.call-done = f32[2048,256]{0,1:T(8,128)} async-done(((f32[2048,256]{0,1:T(8,128)}), f32[2048,256]{0,1:T(8,128)}) %all-reduce.15.cloned.1.call-update) | async-done | bytes 2097168 | tf_op jit(solution)/shard_map/psum | solution.py:14
  1170.5 5.0 fusion.101
  1175.6 58.6 %convolution_bitcast_fusion = f32[4096,256]{0,1:T(8,128)} fusion(f32[2048,256]{1,0:T(8,128)S(1)} %fusion.101, f32[4096,2048]{1,0:T(8,128)} %param.159), kind=kOutput, calls=%fused_computation.205 | convolution fusion | flops 25769803776 | bytes 39845888 | tf_op jit(solution)/shard_map/dot_general | solution.py:18
  1234.2 8.5 fusion.99
  1242.7 32.9 %convolution_bitcast_fusion.1 = f32[2048,256]{0,1:T(8,128)} fusion(f32[4096,256]{1,0:T(8,128)S(1)} %fusion.99, f32[4096,2048]{1,0:T(8,128)} %param.159), kind=kOutput, calls=%fused_computation.221 | convolution fusion | flops 25769803776 | bytes 39845888 | tf_op jit(solution)/shard_map/dot_general | solution.py:18
  1275.6 115.2 %all-reduce.17.cloned.1.call-done = f32[4096,256]{0,1:T(8,128)} async-done(((f32[4096,256]{0,1:T(8,128)}), f32[4096,256]{0,1:T(8,128)}) %all-reduce.17.cloned.1.call-update) | async-done | bytes 4194320 | tf_op jit(solution)/shard_map/psum | solution.py:93
  1390.8 7.7 fusion.222
  1400.6 52.7 %all-reduce.19.cloned.1.call-done = (f32[256,256]{1,0:T(8,128)}, f32[2048,256]{0,1:T(8,128)}) async-done(((f32[256,256]{1,0:T(8,128)}, f32[2048,256]{0,1:T(8,128)}), (f32[256,256]{1,0:T(8,128)}, f32[2048,256]{0,1:T(8,128)})) %all-reduce.19.cloned.1.call-update) | async-done | bytes 2359312 | tf_op jit(solution)/shard_map/psum | solution.py:94
  1454.7 8.2 fusion.83
  1465.9 3.8 fusion.91
  1469.7 59.9 %convolution_subtract_fusion = f32[4096,2048]{1,0:T(8,128)} fusion(f32[4096,2048]{1,0:T(8,128)} %param.159, f32[4096,256]{0,1:T(8,128)} %copy-done.2, f32[4096,256]{0,1:T(8,128)S(1)} %copy-done.1, f32[2048,256]{0,1:T(8,128)S(1)} %copy-done.5, f32[2048,256]{0,1:T(8,128)S(1)} %fusion.91), kind=kOutput, calls=%fused_computation.199 | convolution fusion | flops 51551141888 | bytes 79691776 | tf_op jit(solution)/shard_map/dot_general | solution.py:18
  (2329 shorter events, 441.3 us)
Async XLA Ops:
  7.2 164.2 %all-reduce.9.cloned.1.call-start = ((), (), s32[]{:S(2)}) async-start(), calls=%async_computation | async-start | bytes 8388608 | tf_op jit(solution)/shard_map/psum | solution.py:14
  11.7 203.3 %all-reduce.11.cloned.1.call-start = ((), (), s32[]{:S(2)}) async-start(), calls=%async_computation.1 | async-start | bytes 524288 | tf_op jit(solution)/shard_map/psum | solution.py:77
  183.6 141.9 %all-reduce.13.cloned.1.call-start = ((), (), s32[]{:S(2)}) async-start(), calls=%async_computation.2 | async-start | bytes 524288 | tf_op jit(solution)/shard_map/psum | solution.py:14
  276.9 3.7 copy-start.7
  287.2 4.9 copy-start.8
  290.7 1.3 copy-start.3
  292.1 10.8 copy-start.9
  293.1 877.5 %all-reduce.15.cloned.1.call-start = ((), (), s32[]{:S(2)}) async-start(), calls=%async_computation.3 | async-start | bytes 4194304 | tf_op jit(solution)/shard_map/psum | solution.py:14
  1106.9 1.9 copy-start.4
  1108.9 5.5 copy-start.6
  1115.4 2.0 copy-start
  1118.9 271.9 %all-reduce.17.cloned.1.call-start = ((), (), s32[]{:S(2)}) async-start(), calls=%async_computation.4 | async-start | bytes 8388608 | tf_op jit(solution)/shard_map/psum | solution.py:93
  1234.2 219.2 %all-reduce.19.cloned.1.call-start = ((), (), s32[]{:S(2)}) async-start(), calls=%async_computation.5 | async-start | bytes 4718592 | tf_op jit(solution)/shard_map/psum | solution.py:94
  1454.7 11.2 copy-start.5
  1462.9 2.0 copy-start.2
  1465.9 3.9 copy-start.1
Sparse Core Ops, SparseCore 0:
  12.2 159.0 all-reduce.8
  183.7 31.2 all-reduce.10
  293.2 32.2 all-reduce.12
  1119.1 51.4 all-reduce.14
  1234.3 156.4 all-reduce.16
  1398.7 54.6 all-reduce.18
where the time goes:
time: 1550 us; the launch traced here: 1540 us
  waiting for transfers between devices  402 us (26%)
  loops' own time  341 us (22%)
  local copies, waits for them, and re-layouts  308 us (20%)
  matrix products  243 us (16%)
  other arithmetic  225 us (15%)
  between operations  16.8 us (1%)
    another operation x16, loops' own time, lu_signed(): panel, sign_vec = lax.fori_loop(0, width, leaf_step, (panel, sign_vec))  341 us
    dot_general x25, matrix products, matmul(): jnp.dot(left, right, precision=lax.Precision.HIGHEST, preferred_element_t...  211 us
    psum x3, waiting for transfers between devices, spread(): return lax.psum(kept, axis)  207 us
    dynamic_slice x256, local copies, waits for them, and re-layouts, leaf_step(): raw_pivot = column[pivot_idx]  150 us
    psum x1, waiting for transfers between devices, body(): x_rows = lax.psum(matmul(current, matmul(refl_cols, t_factor)), 'col')  115 us
    psum x1, waiting for transfers between devices, body(): inner_prod = lax.psum(matmul(refl.T, x_rows), 'row')  52.7 us
    scatter x256, other arithmetic, leaf_step(): sign_vec = sign_vec.at[pivot_idx].set(sign_now)  43.6 us
    another operation x6, other arithmetic, body(): chol_low = jnp.linalg.cholesky(gram_sum)  34 us
  transfers between devices with their start and end apart: 6, of which 6 were waited for; matrix products, arithmetic and copies ran while one was open for 5% of the time, Pallas kernels for 0%

commit v1 on v0

v1 whole, which is shorter than its diff:
```python
import functools

import jax
import jax.numpy as jnp
from jax import lax
from jax.experimental import pallas as pl
from jax.experimental.pallas import tpu as pltpu
from jax.sharding import PartitionSpec as P

NB = 256
STRIP = 16


def exact(left, right, dims=((1,), (0,))):
    return lax.dot_general(
        left, right, (dims, ((), ())),
        precision=lax.Precision.HIGHEST, preferred_element_type=jnp.float32,
    )


def split3(left, right, dims=((1,), (0,))):
    return lax.dot_general(
        left, right, (dims, ((), ())),
        precision=lax.Precision.HIGH, preferred_element_type=jnp.float32,
    )


def eliminate(work, held, signed, strip):
    n = work.shape[0]
    lane = lax.broadcasted_iota(jnp.int32, (1, n), 1)
    lanes = lax.broadcasted_iota(jnp.int32, (strip, n), 1)
    subs = lax.broadcasted_iota(jnp.int32, (strip, n), 0)
    signs = jnp.zeros((1, n), jnp.float32)
    held[...] = jnp.zeros_like(held)
    done = []
    for first in range(0, n, strip):
        rows = work[first : first + strip, :]
        forward = rows
        for step in range(strip):
            at = first + step
            row = rows[step : step + 1, :]
            pivot = row[:, at : at + 1]
            if signed:
                sign = jnp.where(pivot >= 0, 1.0, -1.0).astype(jnp.float32)
                pivot = pivot + sign
                signs = jnp.where(lane == at, sign, signs)
            inverse = 1.0 / pivot
            forward = jnp.where(subs == step, jnp.where(lane == at, pivot, row), forward)
            scaled = jnp.where(lane == at, inverse, row * inverse)
            column = rows[:, at : at + 1]
            rest = jnp.where(lanes == at, 0.0, rows) - column * scaled
            rows = jnp.where(subs == step, scaled, rest)
        done.append(forward)
        after = first + strip
        if after < n:
            held[first:after, :] = rows
            below = work[after:, :]
            inside = (lane >= first) & (lane < after)
            lead = jnp.where(inside, below, 0.0)
            work[after:, :] = jnp.where(inside, 0.0, below) - exact(lead, held[...])
            held[first:after, :] = jnp.zeros((strip, n), jnp.float32)
    return jnp.concatenate(done, axis=0), signs


def factor_kernel(strip, gram_ref, top_ref, rinv_ref, lower_ref, linv_ref, uinv_ref, sign_ref,
                  work, held):
    n = gram_ref.shape[0]
    rows = lax.broadcasted_iota(jnp.int32, (n, n), 0)
    cols = lax.broadcasted_iota(jnp.int32, (n, n), 1)
    eye = jnp.where(rows == cols, 1.0, 0.0).astype(jnp.float32)
    work[...] = gram_ref[...]
    packed, _ = eliminate(work, held, False, strip)
    diag = jnp.sum(packed * eye, axis=1, keepdims=True)
    unit_inv = jnp.where(rows > cols, packed, eye)
    chol_inv = unit_inv * (1.0 / jnp.sqrt(diag))
    rinv_ref[...] = chol_inv.T
    top = exact(top_ref[...], rinv_ref[...])
    work[...] = top
    packed, signs = eliminate(work, held, True, strip)
    sign_ref[...] = signs
    linv_ref[...] = jnp.where(rows > cols, packed, eye)
    upper = jnp.where(rows <= cols, packed, 0.0)
    uinv_ref[...] = eye / jnp.sum(packed * eye, axis=1, keepdims=True)
    size = 1
    while size < n:
        mask = ((rows ^ cols) // size == 1) & (cols > rows)
        part = jnp.where(mask, upper, 0.0)
        held_inv = uinv_ref[...]
        uinv_ref[...] = held_inv - exact(exact(held_inv, part), held_inv)
        size *= 2
    low = exact(top + eye * signs, uinv_ref[...])
    lower_ref[...] = jnp.where(rows > cols, low, eye)


def factor(gram, top):
    n = gram.shape[0]
    square = jax.ShapeDtypeStruct((n, n), jnp.float32)
    return pl.pallas_call(
        functools.partial(factor_kernel, STRIP),
        out_shape=[square, square, square, square, jax.ShapeDtypeStruct((1, n), jnp.float32)],
        in_specs=[pl.BlockSpec(memory_space=pltpu.VMEM)] * 2,
        out_specs=[pl.BlockSpec(memory_space=pltpu.VMEM)] * 5,
        scratch_shapes=[pltpu.VMEM((n, n), jnp.float32), pltpu.VMEM((n, n), jnp.float32)],
        compiler_params=pltpu.CompilerParams(vmem_limit_bytes=16 * 1024 * 1024),
        cost_estimate=pl.CostEstimate(flops=20_000_000_000, bytes_accessed=2_000_000, transcendentals=0),
        name="factor",
    )(gram, top)


def body(matrix):
    row_count, col_count = matrix.shape
    n_row, n_col = lax.axis_size("row"), lax.axis_size("col")
    both = ("row", "col")
    share = row_count // n_col
    r, c = lax.axis_index("row"), lax.axis_index("col")
    first = NB
    head = matrix[: 2 * NB, :].T
    col_ids = c * col_count + jnp.arange(col_count)
    panel_own = jnp.where((col_ids >= first)[:, None], head[:, :NB], 0.0)
    next_own = head[:, NB:]
    pieces = [panel_own[k * share : (k + 1) * share] for k in range(n_row)]
    nexts = [next_own[k * share : (k + 1) * share] for k in range(n_row)]
    by_row = sum(
        lax.ppermute(pieces[k], both, [(j, j * n_row + k) for j in range(n_col)])
        for k in range(n_row)
    )

    def to_column_order(parts):
        total = jnp.where(r == 0, parts[0], 0.0)
        for k in range(1, n_row):
            total = total + lax.ppermute(parts[k], "row", [(0, k)])
        return total

    by_col = to_column_order(pieces)
    next_by_col = to_column_order(nexts)
    corner = (r == 0) & (c == 0)
    gram = exact(by_row, by_row, ((0,), (0,)))
    tops = jnp.where(corner, jnp.concatenate([panel_own[first : first + NB], next_own[first : first + NB]]), 0.0)
    small = lax.psum(jnp.concatenate([gram, tops]), both)
    gram_sum, top, next_top = small[:NB], small[NB : 2 * NB], small[2 * NB :]
    rinv, unit_lower, linv, uinv, signs = factor(gram_sum, top)

    panel_rows = lax.all_gather(by_row, "col", axis=0, tiled=True)
    panel_cols = lax.all_gather(by_col, "row", axis=0, tiled=True)
    y_part = split3(matrix, panel_rows, ((0,), (0,)))
    y_top = jnp.where(c == 0, y_part[first : first + NB], 0.0)
    inner = exact(panel_cols, y_part, ((0,), (0,)))
    later, gram_sum = lax.optimization_barrier((jnp.concatenate([inner, y_top]), gram_sum))
    small = lax.psum(later, both)
    inner_sum, y_top = small[:NB], small[NB:]
    y_share = lax.psum_scatter(y_part, "row", scatter_dimension=0, tiled=True)

    scaled_inv = rinv * signs
    x_share = exact(exact(y_share, scaled_inv) + next_by_col, linv, ((1,), (1,)))
    x_share_row = lax.ppermute(
        x_share, both, [(k * n_col + j, j * n_row + k) for k in range(n_row) for j in range(n_col)]
    )
    x_rows = lax.all_gather(x_share_row, "col", axis=0, tiled=True)
    x_cols = lax.all_gather(x_share, "row", axis=0, tiled=True)

    cross = exact(y_top, scaled_inv)
    middle = exact(scaled_inv, exact(inner_sum, scaled_inv), ((0,), (0,))) + cross + cross.T + next_top
    half = 0.5 * exact(linv, exact(middle, linv, ((1,), (1,))))
    shape = exact(rinv, uinv)

    def reflectors(panel, start):
        out = split3(panel, shape)
        rel = start + jnp.arange(panel.shape[0]) - first
        top_rows = jnp.zeros_like(out[: 2 * NB]).at[first:].set(unit_lower)
        in_top = (start == 0) & (rel < NB)
        padded = jnp.concatenate([top_rows, out[2 * NB :]])
        return jnp.where(in_top[:, None], padded, out)

    refl_rows = reflectors(panel_rows, r * row_count)
    refl_cols = reflectors(panel_cols, c * col_count)
    w_rows = x_rows - split3(refl_rows, half)
    w_cols = x_cols - split3(refl_cols, half)
    left = jnp.concatenate([refl_rows, w_rows], axis=1)
    right = jnp.concatenate([w_cols, refl_cols], axis=1)
    updated = matrix - split3(left, right, ((1,), (1,)))
    v_out = lax.dynamic_slice_in_dim(refl_rows, c * share, share, 0)
    w_out = lax.dynamic_slice_in_dim(w_rows, c * share, share, 0)
    return updated, v_out[None], w_out[None]


def solution(mesh):
    return jax.shard_map(
        body,
        mesh=mesh,
        in_specs=(P("row", "col"),),
        out_specs=(P("row", "col"), P(None, ("row", "col"), None), P(None, ("row", "col"), None)),
        check_vma=False,
    )
```

time: 1550 us -> 562 us (0.36)
  loops' own time: 341 us -> 0 us
  local copies, waits for them, and re-layouts: 308 us -> 23.6 us
  other arithmetic: 225 us -> 16.3 us
  matrix products: 243 us -> 81.4 us
  waiting for transfers between devices: 402 us -> 327 us
  Pallas kernels: 0 us -> 60.3 us
  starting transfers between devices: 0.71 us -> 31.2 us
    another operation x19 -> x0, loops' own time: 341 us -> none  [the longest x16 341 us: lu_signed(): panel, sign_vec = lax.fori_loop(0, width, leaf_step, (panel, sign_vec))]
    psum x6 -> x2, waiting for transfers between devices: 402 us -> 219 us  [the longest x1 151 us: body(): small = lax.psum(later, both)]
    dynamic_slice x260 -> x0, local copies, waits for them, and re-layouts: 153 us -> none  [the longest x256 150 us: leaf_step(): raw_pivot = column[pivot_idx]]
    another operation x75 -> x0, other arithmetic: 141 us -> none  [the longest x6 34 us: body(): chol_low = jnp.linalg.cholesky(gram_sum)]
    dot_general x25 -> x16, matrix products: 211 us -> 81.4 us  [the longest x6 64.6 us: split3(): lax.dot_general(left, right, (dims, ((), ())), precision=lax.Precision.HI...]
    all_gather x0 -> x4, waiting for transfers between devices: none -> 94.4 us  [the longest x1 94.4 us: body(): panel_rows = lax.all_gather(by_row, 'col', axis=0, tiled=True)]
    scatter x45 -> x1, local copies, waits for them, and re-layouts: 67.8 us -> 0.04 us  [reflectors(): top_rows = jnp.zeros_like(out[:2 * NB]).at[first:].set(unit_lower)]
    pallas_call x0 -> x1, Pallas kernels: none -> 60.3 us  [factor(): pl.pallas_call(functools.partial(factor_kernel, STRIP), out_shape=[square...]
  transfers between devices with their start and end apart: 6 -> 18, of which waited for: 6 -> 5; matrix products, arithmetic and copies ran while one was open for 5% -> 11% of each run, Pallas kernels for 0% -> 11%
where the time goes in v1:
time: 562 us; the launch traced here: 555 us
  waiting for transfers between devices  327 us (58%)
  matrix products  81.4 us (14%)
  Pallas kernels  60.3 us (11%)
  starting transfers between devices  31.2 us (6%)
  local copies, waits for them, and re-layouts  23.6 us (4%)
  other arithmetic  16.3 us (3%)
  between operations  16.1 us (3%)
    psum x1, waiting for transfers between devices, body(): small = lax.psum(later, both)  151 us
    all_gather x1, waiting for transfers between devices, body(): panel_rows = lax.all_gather(by_row, 'col', axis=0, tiled=True)  94.4 us
    psum x1, waiting for transfers between devices, body(): small = lax.psum(jnp.concatenate([gram, tops]), both)  67.1 us
    dot_general x6, matrix products, split3(): lax.dot_general(left, right, (dims, ((), ())), precision=lax.Precision.HI...  64.6 us
    pallas_call x1, Pallas kernels, factor(): pl.pallas_call(functools.partial(factor_kernel, STRIP), out_shape=[square...  60.3 us
    ppermute x6, starting transfers between devices, to_column_order(): total = total + lax.ppermute(parts[k], 'row', [(0, k)])  17.6 us
    dot_general x10, matrix products, exact(): lax.dot_general(left, right, (dims, ((), ())), precision=lax.Precision.HI...  16.9 us
    ppermute x4, waiting for transfers between devices, body(): lax.ppermute(pieces[k], both, [(j, j * n_row + k) for j in range(n_col)])  12.2 us
  transfers between devices with their start and end apart: 18, of which 5 were waited for; matrix products, arithmetic and copies ran while one was open for 11% of the time, Pallas kernels for 11%

profile of v1, /device:TPU:0, one launch (start us, length us, event | category | flops | bytes accessed | tf_op | source)
XLA Modules:
  0.0 555.4 jit_solution(9011283206484311865)
XLA Ops:
  8.1 4.7 slice.91
  12.8 5.4 copy.10
  18.2 1.8 slice_select_fusion
  19.9 1.2 fusion.35
  21.1 5.1 collective-permute-start.10
  26.3 2.1 collective-permute-start.8
  28.3 2.1 collective-permute-start.9
  30.5 3.4 collective-permute-start.1
  33.9 1.4 collective-permute-start.2
  35.3 2.2 collective-permute-start.3
  38.1 2.3 add_add_fusion
  41.1 12.2 %collective-permute-done.1 = f32[512,256]{1,0:T(8,128)S(1)} collective-permute-done((f32[512,256]{1,0:T(8,128)}, f32[512,256]{1,0:T(8,128)S(1)}, u32[]{:S(2)}, u32[]{:S(2)}) %collective-permute-start.1) | collective-permute-done | bytes 524320 | tf_op jit(solution)/shard_map/ppermute | solution.py:124
  53.2 0.9 add_add_fusion.1
  54.3 1.0 slice.117
  55.3 2.2 fusion.37
  57.5 0.9 pad_maximum_fusion
  58.5 0.7 all-gather.9.cloned.1.call-update
  59.3 94.4 %all-gather.5.cloned.1.call-done = f32[4096,256]{1,0:T(8,128)} async-done(((f32[512,256]{1,0:T(8,128)}), f32[4096,256]{1,0:T(8,128)}) %all-gather.5.cloned.1.call-update) | async-done | bytes 4194320 | tf_op jit(solution)/shard_map/all_gather | solution.py:143
  153.7 19.5 %fusion.40 = f32[256,2048]{1,0:T(8,128)} fusion(f32[4096,256]{1,0:T(8,128)} %all-gather.5.cloned.1.call-done, f32[4096,2048]{1,0:T(8,128)} %param.5), kind=kOutput, calls=%fused_computation.57 | convolution fusion | flops 12884901888 | bytes 39845888 | tf_op jit(solution)/shard_map/dot_general | solution.py:22
  173.3 2.5 fusion.34
  175.8 2.1 collective-permute-start.4
  178.0 3.6 collective-permute-start.5
  181.5 2.6 collective-permute-start.6
  184.1 67.1 %all-reduce.4.cloned.1.call-done = f32[768,256]{1,0:T(8,128)} async-done(((f32[768,256]{1,0:T(8,128)}), f32[768,256]{1,0:T(8,128)}) %all-reduce.4.cloned.1.call-update) | async-done | bytes 786448 | tf_op jit(solution)/shard_map/psum | solution.py:139
  251.2 1.1 fusion.36
  252.2 60.3 %factor.1 = (f32[256,256]{1,0:T(8,128)S(1)}, f32[256,256]{1,0:T(8,128)S(1)}, f32[256,256]{1,0:T(8,128)S(1)}, f32[256,256]{1,0:T(8,128)S(1)}, f32[1,256]{1,0:T(1,128)S(1)}) custom-call(f32[256,256]{1,0:T(8,128)S(1)} %get-tuple-element.44.gram_ref, f32[256,256]{1,0:T(8,128)S(1)} %get-tuple-element.43.top_ref), custom_call_target="tpu_custom_call" | custom-call | flops 20000000000 | bytes 2000000 | tf_op jit(solution)/shard_map/factor/pallas_call | solution.py:98
  312.6 3.6 fusion.41
  316.2 0.9 pad_maximum_fusion.1
  317.2 2.2 fusion.23
  319.4 3.0 fusion.12
  322.4 5.6 %collective-permute-start.7 = (f32[512,256]{1,0:T(8,128)}, f32[512,256]{1,0:T(8,128)}, u32[]{:S(2)}, u32[]{:S(2)}) collective-permute-start(f32[512,256]{1,0:T(8,128)} %fusion.12), channel_id=1, source_target_pairs={{0,0},{1,4},{2,8},{3,12},{4,16},{5,20},{6,24},{7,28},{8,1},{9,5},{... | collective-permute-start | bytes 1572872 | tf_op jit(solution)/shard_map/ppermute | solution.py:155
  328.5 1.0 fusion.44
  330.2 1.5 copy-done.4
  331.8 1.9 fusion.39
  333.9 1.0 maximum_select_fusion
  335.0 2.0 copy-done
  337.0 0.8 dynamic-slice_bitcast_fusion.1
  337.8 151.5 %all-reduce.6.cloned.1.call-done = f32[512,256]{0,1:T(8,128)} async-done(((f32[512,256]{0,1:T(8,128)}), f32[512,256]{0,1:T(8,128)}) %all-reduce.6.cloned.1.call-update) | async-done | bytes 524304 | tf_op jit(solution)/shard_map/psum | solution.py:149
  489.3 1.5 fusion.14
  491.0 1.7 fusion.16
  492.7 1.6 fusion.7
  495.1 2.3 fusion.45
  497.4 3.8 fusion.43
  501.2 3.8 sub.18
  505.0 4.0 sub.16
  509.0 2.0 copy-done.3
  511.0 0.8 dynamic-slice_bitcast_fusion
  511.9 36.0 %convolution_subtract_fusion = f32[4096,2048]{1,0:T(8,128)} fusion(f32[4096,2048]{1,0:T(8,128)} %param.5, f32[4096,256]{1,0:T(8,128)} %copy-done.3, f32[4096,256]{1,0:T(8,128)} %copy-done, f32[2048,256]{1,0:T(8,128)S(1)} %maximum_select_fusion.1, f32[2048,256]{1,0:T(8,128)} %sub.18), kind=kOutput, calls=%fused_computation | convolution fusion | flops 25781338112 | bytes 79691776 | tf_op jit(solution)/shard_map/dot_general | solution.py:22
  (51 shorter events, 4.0 us)
Async XLA Ops:
  8.0 145.7 %all-gather.5.cloned.1.call-start = ((), (), s32[]{:S(2)}) async-start(), calls=%async_computation.2 | async-start | bytes 4718592 | tf_op jit(solution)/shard_map/all_gather | solution.py:143
  21.1 14.2 %collective-permute-start.10 = (f32[512,256]{1,0:T(8,128)}, f32[512,256]{1,0:T(8,128)}, u32[]{:S(2)}, u32[]{:S(2)}) collective-permute-start(f32[512,256]{1,0:T(8,128)} %get-tuple-element.41), channel_id=1, source_target_pairs={{0,24},{1,25},{2,26},{3,27},{4,28},{5,29},{6,30},{7,31}} | collective-permute-start | bytes 1572872 | tf_op jit(solution)/shard_map/ppermute | solution.py:131
  26.3 11.3 %collective-permute-start.8 = (f32[512,256]{1,0:T(8,128)}, f32[512,256]{1,0:T(8,128)}, u32[]{:S(2)}, u32[]{:S(2)}) collective-permute-start(f32[512,256]{1,0:T(8,128)} %get-tuple-element.40), channel_id=1, source_target_pairs={{0,8},{1,9},{2,10},{3,11},{4,12},{5,13},{6,14},{7,15}} | collective-permute-start | bytes 1572872 | tf_op jit(solution)/shard_map/ppermute | solution.py:131
  28.3 9.7 %collective-permute-start.9 = (f32[512,256]{1,0:T(8,128)}, f32[512,256]{1,0:T(8,128)}, u32[]{:S(2)}, u32[]{:S(2)}) collective-permute-start(f32[512,256]{1,0:T(8,128)} %get-tuple-element.42), channel_id=1, source_target_pairs={{0,16},{1,17},{2,18},{3,19},{4,20},{5,21},{6,22},{7,23}} | collective-permute-start | bytes 1572872 | tf_op jit(solution)/shard_map/ppermute | solution.py:131
  30.5 22.8 %collective-permute-start.1 = (f32[512,256]{1,0:T(8,128)}, f32[512,256]{1,0:T(8,128)S(1)}, u32[]{:S(2)}, u32[]{:S(2)}) collective-permute-start(f32[512,256]{1,0:T(8,128)} %get-tuple-element.40), channel_id=1, source_target_pairs={{0,1},{1,5},{2,9},{3,13},{4,17},{5,21},{6,25},{7,29}} | collective-permute-start | bytes 1572872 | tf_op jit(solution)/shard_map/ppermute | solution.py:124
  33.9 19.4 %collective-permute-start.2 = (f32[512,256]{1,0:T(8,128)}, f32[512,256]{1,0:T(8,128)S(1)}, u32[]{:S(2)}, u32[]{:S(2)}) collective-permute-start(f32[512,256]{1,0:T(8,128)} %get-tuple-element.42), channel_id=1, source_target_pairs={{0,2},{1,6},{2,10},{3,14},{4,18},{5,22},{6,26},{7,30}} | collective-permute-start | bytes 1572872 | tf_op jit(solution)/shard_map/ppermute | solution.py:124
  35.3 17.9 %collective-permute-start.3 = (f32[512,256]{1,0:T(8,128)}, f32[512,256]{1,0:T(8,128)S(1)}, u32[]{:S(2)}, u32[]{:S(2)}) collective-permute-start(f32[512,256]{1,0:T(8,128)} %get-tuple-element.41), channel_id=1, source_target_pairs={{0,3},{1,7},{2,11},{3,15},{4,19},{5,23},{6,27},{7,31}} | collective-permute-start | bytes 1572872 | tf_op jit(solution)/shard_map/ppermute | solution.py:124
  40.4 12.9 %collective-permute-start = (f32[512,256]{1,0:T(8,128)S(1)}, f32[512,256]{1,0:T(8,128)S(1)}, u32[]{:S(2)}, u32[]{:S(2)}) collective-permute-start(f32[512,256]{1,0:T(8,128)S(1)} %get-tuple-element.39), channel_id=1, source_target_pairs={{0,0},{1,4},{2,8},{3,12},{4,16},{5,20},{6,24},{7,28}} | collective-permute-start | bytes 1572872 | tf_op jit(solution)/shard_map/ppermute | solution.py:124
  54.2 197.0 %all-reduce.4.cloned.1.call-start = ((), (), s32[]{:S(2)}) async-start(), calls=%async_computation.1 | async-start | bytes 1572864 | tf_op jit(solution)/shard_map/psum | solution.py:139
  58.5 254.1 %all-gather.9.cloned.1.call-start = ((), (), s32[]{:S(2)}) async-start(), calls=%async_computation.5 | async-start | bytes 2621440 | tf_op jit(solution)/shard_map/all_gather | solution.py:144
  59.2 257.9 %reduce-scatter.2.cloned.1.call-start = ((), (), s32[]{:S(2)}) async-start(), calls=%async_computation.3 | async-start | bytes 2621440 | tf_op jit(solution)/shard_map/reduce_scatter | solution.py:151
  173.3 316.0 %all-reduce.6.cloned.1.call-start = ((), (), s32[]{:S(2)}) async-start(), calls=%async_computation.6 | async-start | bytes 1048576 | tf_op jit(solution)/shard_map/psum | solution.py:149
  175.8 143.5 %collective-permute-start.4 = (f32[512,256]{1,0:T(8,128)}, f32[512,256]{1,0:T(8,128)}, u32[]{:S(2)}, u32[]{:S(2)}) collective-permute-start(f32[512,256]{1,0:T(8,128)} %get-tuple-element.35), channel_id=1, source_target_pairs={{0,8},{1,9},{2,10},{3,11},{4,12},{5,13},{6,14},{7,15}} | collective-permute-start | bytes 1572872 | tf_op jit(solution)/shard_map/ppermute | solution.py:131
  178.0 141.4 %collective-permute-start.5 = (f32[512,256]{1,0:T(8,128)}, f32[512,256]{1,0:T(8,128)}, u32[]{:S(2)}, u32[]{:S(2)}) collective-permute-start(f32[512,256]{1,0:T(8,128)} %get-tuple-element.37), channel_id=1, source_target_pairs={{0,16},{1,17},{2,18},{3,19},{4,20},{5,21},{6,22},{7,23}} | collective-permute-start | bytes 1572872 | tf_op jit(solution)/shard_map/ppermute | solution.py:131
  181.5 137.9 %collective-permute-start.6 = (f32[512,256]{1,0:T(8,128)}, f32[512,256]{1,0:T(8,128)}, u32[]{:S(2)}, u32[]{:S(2)}) collective-permute-start(f32[512,256]{1,0:T(8,128)} %get-tuple-element.36), channel_id=1, source_target_pairs={{0,24},{1,25},{2,26},{3,27},{4,28},{5,29},{6,30},{7,31}} | collective-permute-start | bytes 1572872 | tf_op jit(solution)/shard_map/ppermute | solution.py:131
  252.2 60.4 %copy-start.2 = (f32[256,2048]{1,0:T(8,128)S(1)}, f32[256,2048]{1,0:T(8,128)}, u32[]{:S(2)}) copy-start(f32[256,2048]{1,0:T(8,128)} %fusion.40) | copy-start | bytes 6291460
  317.1 11.4 %copy-start.5 = (f32[2048,256]{1,0:T(8,128)S(1)}, f32[2048,256]{1,0:T(8,128)}, u32[]{:S(2)}) copy-start(f32[2048,256]{1,0:T(8,128)} %all-gather.9.cloned.1.call-done) | copy-start | bytes 6291460
  317.1 184.1 %all-gather.11.cloned.1.call-start = ((), (), s32[]{:S(2)}) async-start(), calls=%async_computation.7 | async-start | bytes 2621440 | tf_op jit(solution)/shard_map/all_gather | solution.py:159
  322.4 182.6 %all-gather.7.cloned.1.call-start = ((), (), s32[]{:S(2)}) async-start(), calls=%async_computation.4 | async-start | bytes 4718592 | tf_op jit(solution)/shard_map/all_gather | solution.py:158
  322.4 5.6 %collective-permute-start.7 = (f32[512,256]{1,0:T(8,128)}, f32[512,256]{1,0:T(8,128)}, u32[]{:S(2)}, u32[]{:S(2)}) collective-permute-start(f32[512,256]{1,0:T(8,128)} %fusion.12), channel_id=1, source_target_pairs={{0,0},{1,4},{2,8},{3,12},{4,16},{5,20},{6,24},{7,28},{8,1},{9,5},{... | collective-permute-start | bytes 1572872 | tf_op jit(solution)/shard_map/ppermute | solution.py:155
  329.6 2.2 copy-start.4
  335.0 2.0 copy-start
  491.0 6.4 %copy-start.1 = (f32[4096,256]{1,0:T(8,128)S(1)}, f32[4096,256]{1,0:T(8,128)}, u32[]{:S(2)}) copy-start(f32[4096,256]{1,0:T(8,128)} %copy-done) | copy-start | bytes 12582916
  509.0 2.0 copy-start.3
Sparse Core Ops, SparseCore 0:
  54.3 99.3 all-gather.4
  155.3 21.3 all-gather.8
  179.8 31.1 reduce-scatter.1
  322.5 28.8 all-gather.10
  353.4 81.9 all-gather.6
Sparse Core Ops, SparseCore 1:
  59.9 191.2 all-reduce.3
  317.2 172.0 all-reduce.5
